TPU v7x, 32 devices: a whole 2x2x4 slice. The times are simulated.
32 devices in a mesh: site: 8 (over z, y), rhs: 4 (over x, core).
Axes of the slice: x: 2, y: 2, z: 4, core: 2. Of those that a mesh axis runs over, the one named last changes fastest.
Arguments:
- rhs_vecs: bfloat16 [128, 128, 128], P(None, ('site', 'rhs')), may hold values from -8 to 8, as said below
- deflation: bfloat16 [256, 128, 128], P(None, ('site', 'rhs')), may hold values from -6 to 6
- coarse_inverse: float32 [2, 256, 256], replicated, may hold values from -4.5776367e-05 to 4.5776367e-05
- coupling: bfloat16 [128, 9, 128, 128], P('site'), may hold values from -1 to 5, as said below
- neighbours: int32 [128, 8], P('site'), may hold values from 0 to 127, as said below
- grouping: int32 [128], replicated, may hold values from 0 to 127, each once
Outputs:
- solution: float32 [128, 128, 128], P('rhs', 'site')
- residual: float32 [128, 128, 128], P('rhs', 'site')
Inputs may be any that keep to these rules, and one draw needn't show every extreme that they name: `rhs_vecs`: mean zero, site scales differ from site to site. `coupling`: the self block's real part carries a real diagonal between 2 and 4.2 added to small blocks. Entry m of a site's row lies within 8 positions of the site along the cyclic site order, after it for even m and before it for odd m; in every draw some site has neighbours exactly 8 positions away in both directions.
All inputs are finite; a program needn't handle non-finite values.
Results may differ from a plain program's by a relative error of at most 0.01.
Values may be sent and summed in bfloat16 or wider, within the bound.
A program may use at most 64 MiB of HBM per device.

v0:
```python
import jax
import jax.numpy as jnp
from jax import lax
from jax.sharding import PartitionSpec as P

MR_STEPS = 2


def extended_2(array, sides, width):
    for axis, dim in sides:
        size, length = (lax.axis_size(axis), array.shape[dim])
        up = [(i, (i + 1) % size) for i in range(size)]
        down = [(j, i) for i, j in up]
        last = lax.slice_in_dim(array, length - width, length, axis=dim)
        first = lax.slice_in_dim(array, 0, width, axis=dim)
        before = lax.ppermute(last, axis, up)
        after = lax.ppermute(first, axis, down)
        array = jnp.concatenate([before, array, after], axis=dim)
    return array


def turned(vectors):
    half_width = vectors.shape[-1] // 2
    return jnp.concatenate([-vectors[..., half_width:], vectors[..., :half_width]], axis=-1)


def conj_turned(vectors):
    half_width = vectors.shape[-1] // 2
    return jnp.concatenate([vectors[..., half_width:], -vectors[..., :half_width]], axis=-1)


def scaled(alpha_re, alpha_im, vectors):
    return alpha_re[:, None, None] * vectors + alpha_im[:, None, None] * turned(vectors)


def small_solve(coarse_inverse, coef_re, coef_im):
    highest = lax.Precision.HIGHEST
    real_part = coarse_inverse[0]
    imag_part = coarse_inverse[1]
    solved_re = jnp.dot(
        real_part, coef_re, precision=highest, preferred_element_type=jnp.float32
    ) - jnp.dot(imag_part, coef_im, precision=highest, preferred_element_type=jnp.float32)
    solved_im = jnp.dot(
        real_part, coef_im, precision=highest, preferred_element_type=jnp.float32
    ) + jnp.dot(imag_part, coef_re, precision=highest, preferred_element_type=jnp.float32)
    return (solved_re, solved_im)


def operate(vectors, coupling, neighbours):
    slots = vectors.shape[0]
    sites_here = vectors.shape[1]
    width = vectors.shape[2]
    reach = sites_here // 2
    extended = extended_2(vectors, (("site", 1),), reach)
    anchor = lax.axis_index("site") * sites_here
    total = sites_here * lax.axis_size("site")
    position = (neighbours - anchor + reach) % total
    beside = jnp.take(extended, position.reshape(-1), axis=1).reshape(slots, sites_here, 8, width)
    stacked = jnp.concatenate([vectors[:, :, None, :], beside], axis=2).reshape(
        slots, sites_here, 9 * width
    )
    blocks = coupling.reshape(sites_here, 9 * width, width)
    product = lax.dot_general(
        stacked, blocks, (((2,), (1,)), ((1,), (0,))), preferred_element_type=jnp.float32
    )
    return jnp.transpose(product, (1, 0, 2))


def per_device(rhs_vecs, deflation, coarse_inverse, coupling, neighbours, grouping):
    ordered = jnp.take(rhs_vecs, grouping, axis=0)
    coef_re = jnp.einsum("ksc,rsc->kr", deflation, ordered, preferred_element_type=jnp.float32)
    coef_im = jnp.einsum(
        "ksc,rsc->kr", deflation, conj_turned(ordered), preferred_element_type=jnp.float32
    )
    group_re, group_im = (
        lax.psum_scatter(coef_re, "rhs", scatter_dimension=1, tiled=True),
        lax.psum_scatter(coef_im, "rhs", scatter_dimension=1, tiled=True),
    )
    group_re, group_im = lax.psum((group_re, group_im), "site")
    share_re, share_im = small_solve(coarse_inverse, group_re, group_im)
    solved_re, solved_im = (
        lax.all_gather(share_re.astype(jnp.bfloat16), "rhs", axis=1, tiled=True).astype(
            share_re.dtype
        ),
        lax.all_gather(share_im.astype(jnp.bfloat16), "rhs", axis=1, tiled=True).astype(
            share_im.dtype
        ),
    )
    low_re = solved_re.astype(jnp.bfloat16)
    low_im = solved_im.astype(jnp.bfloat16)
    start = jnp.einsum("kr,ksc->rsc", low_re, deflation, preferred_element_type=jnp.float32)
    start = start + jnp.einsum(
        "kr,ksc->rsc", low_im, turned(deflation), preferred_element_type=jnp.float32
    )
    start_low = start.astype(jnp.bfloat16)
    given_low, placed = (
        lax.all_to_all(ordered, "rhs", split_axis=0, concat_axis=1, tiled=True),
        lax.all_to_all(start_low, "rhs", split_axis=0, concat_axis=1, tiled=True),
    )
    given = given_low.astype(jnp.float32)
    solution = placed.astype(jnp.float32)
    residual = given - operate(placed, coupling, neighbours)
    for iteration in range(MR_STEPS):
        image = operate(residual.astype(jnp.bfloat16), coupling, neighbours)
        upper_re = jnp.sum(image * residual, axis=(1, 2))
        upper_im = jnp.sum(image * conj_turned(residual), axis=(1, 2))
        lower = jnp.sum(image * image, axis=(1, 2))
        upper_re, upper_im, lower = lax.psum((upper_re, upper_im, lower), "site")
        alpha_re = upper_re / lower
        alpha_im = upper_im / lower
        solution = solution + scaled(alpha_re, alpha_im, residual)
        residual = residual - scaled(alpha_re, alpha_im, image)
    return (solution, residual)


def solution(mesh):
    return jax.shard_map(
        per_device,
        mesh=mesh,
        in_specs=(
            P(None, ("site", "rhs"), None),
            P(None, ("site", "rhs"), None),
            P(),
            P("site", None, None, None),
            P("site", None),
            P(),
        ),
        out_specs=(P("rhs", "site", None), P("rhs", "site", None)),
        check_vma=False,
    )
```

profile of v0, /device:TPU:0, one launch (start us, length us, event | category | flops | bytes accessed | tf_op | source)
XLA Modules:
  0.0 253.1 jit_solution(11667804039437878166)
XLA Ops:
  9.5 1.8 convolution_bitcast_fusion.1
  11.5 1.8 convolution_bitcast_fusion
  13.8 20.0 %reduce-scatter.3.cloned.1.call-done = f32[256,32]{0,1:T(8,128)} async-done(((f32[256,128]{0,1:T(8,128)}), f32[256,32]{0,1:T(8,128)}) %reduce-scatter.3.cloned.1.call-update) | async-done | bytes 32784 | tf_op jit(solution)/shard_map/reduce_scatter | solution.py:76
  33.9 22.6 %reduce-scatter.5.cloned.1.call-done = f32[256,32]{0,1:T(8,128)} async-done(((f32[256,128]{0,1:T(8,128)}), f32[256,32]{0,1:T(8,128)}) %reduce-scatter.5.cloned.1.call-update) | async-done | bytes 32784 | tf_op jit(solution)/shard_map/reduce_scatter | solution.py:77
  56.6 73.0 %all-reduce.5.cloned.1.call-done = (f32[256,32]{0,1:T(8,128)}, f32[256,32]{0,1:T(8,128)}) async-done(((f32[256,32]{0,1:T(8,128)}, f32[256,32]{0,1:T(8,128)}), (f32[256,32]{0,1:T(8,128)}, f32[256,32]{0,1:T(8,128)})) %all-reduce.5.cloned.1.call-update) | async-done | bytes 65552 | tf_op jit(solution)/shard_map/psum | solution.py:79
  129.6 1.1 fusion.40
  130.7 1.1 fusion.38
  131.8 1.1 fusion.22
  132.9 1.1 fusion.21
  134.0 5.2 %all_gather.7 = bf16[256,128]{0,1:T(8,128)(2,1)S(1)} all-gather(bf16[256,32]{0,1:T(8,128)(2,1)S(1)} %fusion.21), channel_id=1, replica_groups=mesh['site'=8,'rhs'=4] {'rhs'}, dimensions={1}, use_global_device_ids=true | all-gather | bytes 81920 | tf_op jit(solution)/shard_map/all_gather | solution.py:85
  139.2 5.2 %all_gather.6 = bf16[256,128]{0,1:T(8,128)(2,1)S(1)} all-gather(bf16[256,32]{0,1:T(8,128)(2,1)S(1)} %fusion.22), channel_id=1, replica_groups=mesh['site'=8,'rhs'=4] {'rhs'}, dimensions={1}, use_global_device_ids=true | all-gather | bytes 81920 | tf_op jit(solution)/shard_map/all_gather | solution.py:82
  145.7 3.3 %all-to-all-start = ((bf16[128,4,128]{2,1,0:T(4,128)(2,1)}), bf16[128,4,128]{2,1,0:T(4,128)(2,1)S(1)}, u32[]{:S(2)}, u32[]{:S(2)}) async-start(bf16[128,4,128]{2,1,0:T(4,128)(2,1)} %copy.70), calls=%async_computation.2 | async-start | bytes 262144 | tf_op jit(solution)/shard_map/all_to_all | solution.py:98
  149.8 3.8 %all-to-all-done = bf16[128,4,128]{2,1,0:T(4,128)(2,1)S(1)} async-done(((bf16[128,4,128]{2,1,0:T(4,128)(2,1)}), bf16[128,4,128]{2,1,0:T(4,128)(2,1)S(1)}, u32[]{:S(2)}, u32[]{:S(2)}) %all-to-all-start) | async-done | bytes 131104 | tf_op jit(solution)/shard_map/all_to_all | solution.py:98
  153.6 3.3 %all-to-all-start.1 = ((bf16[128,4,128]{2,1,0:T(4,128)(2,1)}), bf16[128,4,128]{2,1,0:T(4,128)(2,1)S(1)}, u32[]{:S(2)}, u32[]{:S(2)}) async-start(bf16[128,4,128]{2,1,0:T(4,128)(2,1)} %copy.73), calls=%async_computation.3 | async-start | bytes 262144 | tf_op jit(solution)/shard_map/all_to_all | solution.py:97
  157.0 1.5 collective-permute-start
  158.5 3.3 %collective-permute-start.1 = (bf16[32,8,128]{2,0,1:T(8,128)(2,1)S(1)}, bf16[32,8,128]{2,0,1:T(8,128)(2,1)S(1)}, u32[]{:S(2)}, u32[]{:S(2)}) collective-permute-start(bf16[32,8,128]{2,0,1:T(8,128)(2,1)S(1)} %get-tuple-element.48), channel_id=1, source_target_pairs={{4,0},{8,4},{12,8},{16,12},{20,16},{24,20},{28,24},{0,28},{5,1},{9... | collective-permute-start | bytes 196616 | tf_op jit(solution)/shard_map/ppermute | solution.py:17
  162.7 1.5 collective-permute-done
  165.6 0.9 pad_maximum_fusion
  167.2 3.4 %fusion.68 = (bf16[32,16,128]{2,0,1:T(8,128)(2,1)S(1)}, f32[32,16,128]{2,0,1:T(8,128)S(1)}) fusion(f32[32,16,128]{2,0,1:T(8,128)} %bitcast.78, bf16[16,1152,128]{2,1,0:T(8,128)(2,1)} %bitcast.67, bf16[32,16,1152]{2,1,0:T(8,128)(2,1)S(1)} %reshape.53), kind=kOutput, calls=%fused_computation.105 | convolution fusion | flops 151126016 | bytes 6553600 | tf_op jit(solution)/shard_map/dot_general | solution.py:63
  170.6 1.2 collective-permute-start.2
  171.8 3.6 %collective-permute-start.3 = (bf16[32,8,128]{2,0,1:T(8,128)(2,1)S(1)}, bf16[32,8,128]{2,0,1:T(8,128)(2,1)S(1)}, u32[]{:S(2)}, u32[]{:S(2)}) collective-permute-start(bf16[32,8,128]{2,0,1:T(8,128)(2,1)S(1)} %get-tuple-element.46), channel_id=1, source_target_pairs={{4,0},{8,4},{12,8},{16,12},{20,16},{24,20},{28,24},{0,28},{5,1},{9... | collective-permute-start | bytes 196616 | tf_op jit(solution)/shard_map/ppermute | solution.py:17
  175.4 0.9 fusion.61
  176.4 1.2 collective-permute-done.2
  179.9 1.5 reshape.56
  181.4 3.8 %multiply_reduce_fusion.3 = (f32[32]{0:T(128)S(1)}, f32[32]{0:T(128)S(1)}, f32[32]{0:T(128)S(1)}, f32[32,16,128]{2,0,1:T(8,128)S(1)}) fusion(f32[32,16,128]{2,0,1:T(8,128)S(1)} %get-tuple-element.56, f32[32,16,64]{2,0,1:T(8,128)S(1)} %get-tuple-element.37, f32[32,16,64]{2,0,1:T(8,128)S(1)} %get-tuple-element.35, bf16[16,1152,128]{2,1,0:T(8,128)(2,1)} %bitcast.68, ...), kind=kOutput, calls=%fused_computation.64 | convolution fusion | flops 151453600 | bytes 6685056 | tf_op jit(solution)/shard_map/dot_general | solution.py:63
  185.4 21.8 %all-reduce.1 = (f32[32]{0:T(128)S(1)}, f32[32]{0:T(128)S(1)}, f32[32]{0:T(128)S(1)}) all-reduce(f32[32]{0:T(128)S(1)} %get-tuple-element.15, f32[32]{0:T(128)S(1)} %get-tuple-element.16, f32[32]{0:T(128)S(1)} %get-tuple-element.14), channel_id=1, replica_groups=mesh['site'=8,'rhs'=4] {'site'}, use_global_device_ids=true, to_apply=%region_9.11 | all-reduce | flops 96 | bytes 768 | tf_op jit(solution)/shard_map/psum | solution.py:108
  207.5 4.7 %collective-permute-start.5 = (bf16[32,8,128]{2,0,1:T(8,128)(2,1)S(1)}, bf16[32,8,128]{2,0,1:T(8,128)(2,1)S(1)}, u32[]{:S(2)}, u32[]{:S(2)}) collective-permute-start(bf16[32,8,128]{2,0,1:T(8,128)(2,1)S(1)} %get-tuple-element.44), channel_id=1, source_target_pairs={{4,0},{8,4},{12,8},{16,12},{20,16},{24,20},{28,24},{0,28},{5,1},{9... | collective-permute-start | bytes 196616 | tf_op jit(solution)/shard_map/ppermute | solution.py:17
  212.2 0.9 fusion.60
  213.1 0.9 copy.83
  217.1 1.5 reshape.58
  218.6 3.9 %multiply_reduce_fusion.1 = (f32[32]{0:T(128)S(1)}, f32[32]{0:T(128)S(1)}, f32[32]{0:T(128)S(1)}, f32[32,16,128]{2,0,1:T(8,128)S(1)}) fusion(f32[32,16,128]{2,0,1:T(8,128)S(1)} %get-tuple-element.26, f32[32,16,64]{2,0,1:T(8,128)S(1)} %get-tuple-element.32, f32[32,16,64]{2,0,1:T(8,128)S(1)} %get-tuple-element.31, bf16[16,1152,128]{2,1,0:T(8,128)(2,1)} %bitcast.69, ...), kind=kOutput, calls=%fused_computation.62 | convolution fusion | flops 151453600 | bytes 6685056 | tf_op jit(solution)/shard_map/dot_general | solution.py:63
  222.7 21.8 %all-reduce = (f32[32]{0:T(128)S(1)}, f32[32]{0:T(128)S(1)}, f32[32]{0:T(128)S(1)}) all-reduce(f32[32]{0:T(128)S(1)} %get-tuple-element.12, f32[32]{0:T(128)S(1)} %get-tuple-element.13, f32[32]{0:T(128)S(1)} %get-tuple-element.11), channel_id=1, replica_groups=mesh['site'=8,'rhs'=4] {'site'}, use_global_device_ids=true, to_apply=%region_15.17 | all-reduce | flops 96 | bytes 768 | tf_op jit(solution)/shard_map/psum | solution.py:108
  (79 shorter events, 16.1 us)
Async XLA Ops:
  7.2 1.5 copy-start
  7.2 6.3 %copy-start.1 = (bf16[256,4,128]{2,1,0:T(4,128)(2,1)S(1)}, bf16[256,4,128]{2,1,0:T(4,128)(2,1)}, u32[]{:S(2)}) copy-start(bf16[256,4,128]{2,1,0:T(4,128)(2,1)} %param.9) | copy-start | bytes 786436
  7.2 6.3 %copy-start.8 = (s32[16,8]{0,1:T(8,128)S(1)}, s32[16,8]{0,1:T(8,128)}, u32[]{:S(2)}) copy-start(s32[16,8]{0,1:T(8,128)} %param.12) | copy-start | bytes 1540
  7.2 26.7 %reduce-scatter.3.cloned.1.call-start = ((), (), s32[]{:S(2)}) async-start(), calls=%async_computation.4 | async-start | bytes 163840 | tf_op jit(solution)/shard_map/reduce_scatter | solution.py:76
  8.6 120.9 %copy-start.2 = (f32[2,256,256]{2,1,0:T(8,128)S(1)}, f32[2,256,256]{2,1,0:T(8,128)}, u32[]{:S(2)}) copy-start(f32[2,256,256]{2,1,0:T(8,128)} %param.10) | copy-start | bytes 1572868
  11.4 45.2 %reduce-scatter.5.cloned.1.call-start = ((), (), s32[]{:S(2)}) async-start(), calls=%async_computation.5 | async-start | bytes 163840 | tf_op jit(solution)/shard_map/reduce_scatter | solution.py:77
  13.4 116.2 %all-reduce.5.cloned.1.call-start = ((), (), s32[]{:S(2)}) async-start(), calls=%async_computation.6 | async-start | bytes 131072 | tf_op jit(solution)/shard_map/psum | solution.py:79
  145.7 7.9 %all-to-all-start = ((bf16[128,4,128]{2,1,0:T(4,128)(2,1)}), bf16[128,4,128]{2,1,0:T(4,128)(2,1)S(1)}, u32[]{:S(2)}, u32[]{:S(2)}) async-start(bf16[128,4,128]{2,1,0:T(4,128)(2,1)} %copy.70), calls=%async_computation.2 | async-start | bytes 262144 | tf_op jit(solution)/shard_map/all_to_all | solution.py:98
  153.6 8.2 %all-to-all-start.1 = ((bf16[128,4,128]{2,1,0:T(4,128)(2,1)}), bf16[128,4,128]{2,1,0:T(4,128)(2,1)S(1)}, u32[]{:S(2)}, u32[]{:S(2)}) async-start(bf16[128,4,128]{2,1,0:T(4,128)(2,1)} %copy.73), calls=%async_computation.3 | async-start | bytes 262144 | tf_op jit(solution)/shard_map/all_to_all | solution.py:97
  157.0 7.2 %collective-permute-start = (bf16[32,8,128]{2,0,1:T(8,128)(2,1)S(1)}, bf16[32,8,128]{2,0,1:T(8,128)(2,1)S(1)}, u32[]{:S(2)}, u32[]{:S(2)}) collective-permute-start(bf16[32,8,128]{2,0,1:T(8,128)(2,1)S(1)} %get-tuple-element.47), channel_id=1, source_target_pairs={{0,4},{4,8},{8,12},{12,16},{16,20},{20,24},{24,28},{28,0},{1,5},{5... | collective-permute-start | bytes 196616 | tf_op jit(solution)/shard_map/ppermute | solution.py:16
  158.5 5.7 %collective-permute-start.1 = (bf16[32,8,128]{2,0,1:T(8,128)(2,1)S(1)}, bf16[32,8,128]{2,0,1:T(8,128)(2,1)S(1)}, u32[]{:S(2)}, u32[]{:S(2)}) collective-permute-start(bf16[32,8,128]{2,0,1:T(8,128)(2,1)S(1)} %get-tuple-element.48), channel_id=1, source_target_pairs={{4,0},{8,4},{12,8},{16,12},{20,16},{24,20},{28,24},{0,28},{5,1},{9... | collective-permute-start | bytes 196616 | tf_op jit(solution)/shard_map/ppermute | solution.py:17
  170.6 7.0 %collective-permute-start.2 = (bf16[32,8,128]{2,0,1:T(8,128)(2,1)S(1)}, bf16[32,8,128]{2,0,1:T(8,128)(2,1)S(1)}, u32[]{:S(2)}, u32[]{:S(2)}) collective-permute-start(bf16[32,8,128]{2,0,1:T(8,128)(2,1)S(1)} %get-tuple-element.45), channel_id=1, source_target_pairs={{0,4},{4,8},{8,12},{12,16},{16,20},{20,24},{24,28},{28,0},{1,5},{5... | collective-permute-start | bytes 196616 | tf_op jit(solution)/shard_map/ppermute | solution.py:16
  171.8 5.8 %collective-permute-start.3 = (bf16[32,8,128]{2,0,1:T(8,128)(2,1)S(1)}, bf16[32,8,128]{2,0,1:T(8,128)(2,1)S(1)}, u32[]{:S(2)}, u32[]{:S(2)}) collective-permute-start(bf16[32,8,128]{2,0,1:T(8,128)(2,1)S(1)} %get-tuple-element.46), channel_id=1, source_target_pairs={{4,0},{8,4},{12,8},{16,12},{20,16},{24,20},{28,24},{0,28},{5,1},{9... | collective-permute-start | bytes 196616 | tf_op jit(solution)/shard_map/ppermute | solution.py:17
  207.5 7.0 %collective-permute-start.4 = (bf16[32,8,128]{2,0,1:T(8,128)(2,1)S(1)}, bf16[32,8,128]{2,0,1:T(8,128)(2,1)S(1)}, u32[]{:S(2)}, u32[]{:S(2)}) collective-permute-start(bf16[32,8,128]{2,0,1:T(8,128)(2,1)S(1)} %get-tuple-element.43), channel_id=1, source_target_pairs={{0,4},{4,8},{8,12},{12,16},{16,20},{20,24},{24,28},{28,0},{1,5},{5... | collective-permute-start | bytes 196616 | tf_op jit(solution)/shard_map/ppermute | solution.py:16
  207.5 7.0 %collective-permute-start.5 = (bf16[32,8,128]{2,0,1:T(8,128)(2,1)S(1)}, bf16[32,8,128]{2,0,1:T(8,128)(2,1)S(1)}, u32[]{:S(2)}, u32[]{:S(2)}) collective-permute-start(bf16[32,8,128]{2,0,1:T(8,128)(2,1)S(1)} %get-tuple-element.44), channel_id=1, source_target_pairs={{4,0},{8,4},{12,8},{16,12},{20,16},{24,20},{28,24},{0,28},{5,1},{9... | collective-permute-start | bytes 196616 | tf_op jit(solution)/shard_map/ppermute | solution.py:17
  215.3 1.0 copy-start.7
  218.6 25.9 %copy-start.3 = (f32[32,16,64]{2,0,1:T(8,128)S(1)}, f32[32,16,64]{2,0,1:T(8,128)}, u32[]{:S(2)}) copy-start(f32[32,16,64]{2,0,1:T(8,128)} %get-tuple-element.36) | copy-start | bytes 393220
  218.6 25.9 %copy-start.4 = (f32[32,16,64]{2,0,1:T(8,128)S(1)}, f32[32,16,64]{2,0,1:T(8,128)}, u32[]{:S(2)}) copy-start(f32[32,16,64]{2,0,1:T(8,128)} %get-tuple-element.38) | copy-start | bytes 393220
  218.6 25.9 %copy-start.5 = (f32[32,16,64]{2,0,1:T(8,128)S(1)}, f32[32,16,64]{2,0,1:T(8,128)}, u32[]{:S(2)}) copy-start(f32[32,16,64]{2,0,1:T(8,128)} %get-tuple-element.33) | copy-start | bytes 393220
  218.6 25.9 %copy-start.6 = (f32[32,16,64]{2,0,1:T(8,128)S(1)}, f32[32,16,64]{2,0,1:T(8,128)}, u32[]{:S(2)}) copy-start(f32[32,16,64]{2,0,1:T(8,128)} %get-tuple-element.34) | copy-start | bytes 393220
Sparse Core Ops, SparseCore 0:
  11.5 22.3 reduce-scatter.2
  36.9 19.6 reduce-scatter.4
  60.1 69.4 all-reduce.4
where the time goes:
time: 254 us; the launch traced here: 253 us
  waiting for transfers between devices  123 us (48%)
  blocking collectives  54.1 us (21%)
  starting transfers between devices  21.1 us (8%)
  matrix products  19.7 us (8%)
  between operations  14.2 us (6%)
  local copies, waits for them, and re-layouts  13.8 us (5%)
  other arithmetic  7.58 us (3%)
    psum x1, waiting for transfers between devices, per_device(): group_re, group_im = lax.psum((group_re, group_im), 'site')  73 us
    psum x2, blocking collectives, per_device(): upper_re, upper_im, lower = lax.psum((upper_re, upper_im, lower), 'site')  43.7 us
    reduce_scatter x1, waiting for transfers between devices, per_device(): lax.psum_scatter(coef_im, 'rhs', scatter_dimension=1, tiled=True)  22.6 us
    reduce_scatter x1, waiting for transfers between devices, per_device(): lax.psum_scatter(coef_re, 'rhs', scatter_dimension=1, tiled=True)  20 us
    ppermute x3, starting transfers between devices, extended_2(): after = lax.ppermute(first, axis, down)  11.5 us
    dot_general x3, matrix products, operate(): lax.dot_general(stacked, blocks, (((2,), (1,)), ((1,), (0,))), preferred_...  11.1 us
    all_gather x1, blocking collectives, per_device(): lax.all_gather(share_im.astype(jnp.bfloat16), 'rhs', axis=1, tiled=True)  5.24 us
    all_gather x1, blocking collectives, per_device(): lax.all_gather(share_re.astype(jnp.bfloat16), 'rhs', axis=1, tiled=True)  5.22 us
  transfers between devices with their start and end apart: 11, of which 7 were waited for; matrix products, arithmetic and copies ran while one was open for 3% of the time, Pallas kernels for 0%

commit v1 on v0

--- a/solution.py
+++ b/solution.py
@@ -1,8 +1,13 @@
+import functools
+
 import jax
 import jax.numpy as jnp
 from jax import lax
+from jax.experimental import pallas as pl
+from jax.experimental.pallas import tpu as pltpu
 from jax.sharding import PartitionSpec as P
 
+MESH = pl.DeviceIdType.MESH
 MR_STEPS = 2
 
 
@@ -66,7 +71,7 @@
     return jnp.transpose(product, (1, 0, 2))
 
 
-def per_device(rhs_vecs, deflation, coarse_inverse, coupling, neighbours, grouping):
+def staged(rhs_vecs, deflation, coarse_inverse, coupling, neighbours, grouping):
     ordered = jnp.take(rhs_vecs, grouping, axis=0)
     coef_re = jnp.einsum("ksc,rsc->kr", deflation, ordered, preferred_element_type=jnp.float32)
     coef_im = jnp.einsum(
@@ -113,9 +118,306 @@
     return (solution, residual)
 
 
+def lanes_turned(values, conj):
+    width = values.shape[-1]
+    lane = lax.broadcasted_iota(jnp.int32, values.shape, values.ndim - 1)
+    rolled = pltpu.roll(values, width // 2, values.ndim - 1)
+    low = lane < width // 2
+    if conj:
+        return jnp.where(low, rolled, -rolled)
+    return jnp.where(low, -rolled, rolled)
+
+
+def fused_kernel(
+    n_site, n_rhs,
+    rhs_ref, defl_ref, inv_ref, coup_hbm, nb_ref, group_ref,
+    sol_ref, res_ref,
+    coup, gathered, ordered, given, coef, parts, solved, solved_all, ext0, ext1, ext2, image, sums, sums_all,
+    coup_sem, coef_send, coef_recv, pack_send, pack_recv, defl_send, defl_recv,
+    solved_send, solved_recv, halo_send, halo_recv, sums_send, sums_recv,
+):
+    devices = n_site * n_rhs
+    sites_local, slots, width = rhs_ref.shape
+    sites_here = coup_hbm.shape[0]
+    reach = sites_here // 2
+    group = slots // n_rhs
+    share = group // n_site
+    vecs = defl_ref.shape[1]
+    f32, bf16 = jnp.float32, jnp.bfloat16
+    exts = (ext0, ext1, ext2)
+
+    my_site = lax.axis_index("site")
+    my_rhs = lax.axis_index("rhs")
+    me = my_rhs * n_site + my_site
+
+    def peer(d):
+        at = lax.rem(me + d, devices)
+        return at, (lax.rem(at, n_site), at // n_site)
+
+    barrier = pltpu.get_barrier_semaphore()
+
+    def greet(d, carry):
+        _, dev = peer(d)
+        pl.semaphore_signal(barrier, inc=1, device_id=dev, device_id_type=MESH)
+        return carry
+
+    lax.fori_loop(1, devices, greet, 0)
+    load_coup = pltpu.make_async_copy(coup_hbm, coup, coup_sem)
+    load_coup.start()
+
+    row = lax.broadcasted_iota(jnp.int32, (slots, slots), 0)
+    placed = jnp.where(row == group_ref[...], 1.0, 0.0).astype(f32)
+    placed = jnp.transpose(placed).astype(bf16)
+    row2 = lax.broadcasted_iota(jnp.int32, (2 * slots, slots), 0)
+    col2 = lax.broadcasted_iota(jnp.int32, (2 * slots, slots), 1)
+    spread = jnp.where(col2 == (row2 // (2 * share)) * share + row2 % share, 1.0, 0.0).astype(bf16)
+    part = (lax.broadcasted_iota(jnp.int32, (2 * slots, width), 0) // share) % 2
+    both = []
+    for i in range(sites_local):
+        g = jnp.dot(placed, rhs_ref[i], preferred_element_type=f32).astype(bf16)
+        ordered[i] = g
+        two = jnp.dot(spread, g, preferred_element_type=f32)
+        both.append(jnp.where(part == 1, lanes_turned(two, True), two).astype(bf16))
+    both = jnp.concatenate(both, axis=1)
+    basis = jnp.concatenate([defl_ref[i] for i in range(sites_local)], axis=1)
+    total = lax.dot_general(both, basis, (((1,), (1,)), ((), ())), preferred_element_type=f32)
+    coef[...] = total.reshape(devices, 2 * share, vecs)
+
+    pl.semaphore_wait(barrier, devices - 1)
+
+    def coef_copy(d):
+        at, dev = peer(d)
+        return pltpu.make_async_remote_copy(
+            src_ref=coef.at[at], dst_ref=parts.at[me], send_sem=coef_send.at[d],
+            recv_sem=coef_recv.at[me], device_id=dev, device_id_type=MESH)
+
+    def coef_start(d, carry):
+        coef_copy(d).start()
+        return carry
+
+    lax.fori_loop(1, devices, coef_start, 0)
+
+    packs, defls = [], []
+    for d in range(1, n_rhs):
+        other = lax.rem(my_rhs + d, n_rhs)
+        packs.append(pltpu.make_async_remote_copy(
+            src_ref=ordered.at[:, pl.ds(pl.multiple_of(other * group, group), group), :],
+            dst_ref=given.at[pl.ds(my_rhs * sites_local, sites_local)],
+            send_sem=pack_send.at[d], recv_sem=pack_recv.at[d],
+            device_id=(my_site, other), device_id_type=MESH))
+        defls.append(pltpu.make_async_remote_copy(
+            src_ref=defl_ref,
+            dst_ref=gathered.at[pl.ds(my_rhs * sites_local, sites_local)],
+            send_sem=defl_send.at[d], recv_sem=defl_recv.at[d],
+            device_id=(my_site, other), device_id_type=MESH))
+    for copy in packs + defls:
+        copy.start()
+    given[pl.ds(my_rhs * sites_local, sites_local)] = ordered[:, pl.ds(pl.multiple_of(my_rhs * group, group), group), :]
+    gathered[pl.ds(my_rhs * sites_local, sites_local)] = defl_ref[...]
+    parts[me] = coef[me]
+
+    def coef_wait(d, carry):
+        at, dev = peer(d)
+        pltpu.make_async_remote_copy(
+            src_ref=coef.at[at], dst_ref=parts.at[at], send_sem=coef_send.at[d],
+            recv_sem=coef_recv.at[at], device_id=dev, device_id_type=MESH).wait_recv()
+        return carry
+
+    lax.fori_loop(1, devices, coef_wait, 0)
+    mine = jnp.sum(parts[...], axis=0)
+    swapped = pltpu.roll(mine, share, 0)
+    first = lax.broadcasted_iota(jnp.int32, mine.shape, 0) < share
+    swapped = jnp.where(first, -swapped, swapped)
+    nt = (((1,), (1,)), ((), ()))
+    out = lax.dot_general(mine, inv_ref[0], nt, precision=lax.Precision.HIGHEST, preferred_element_type=f32)
+    out = out + lax.dot_general(swapped, inv_ref[1], nt, precision=lax.Precision.HIGHEST, preferred_element_type=f32)
+    solved[...] = out
+
+    def along(d):
+        return lax.rem(my_site + d, n_site)
+
+    def to_all_sites(src, dst, send, recv):
+        copies = []
+        for d in range(1, n_site):
+            copies.append(pltpu.make_async_remote_copy(
+                src_ref=src, dst_ref=dst.at[my_site], send_sem=send.at[d],
+                recv_sem=recv.at[d], device_id=(along(d), my_rhs), device_id_type=MESH))
+        for copy in copies:
+            copy.start()
+        dst[my_site] = src[...]
+        return copies
+
+    copies = to_all_sites(solved, solved_all, solved_send, solved_recv)
+
+    def coef_sent(d, carry):
+        coef_copy(d).wait_send()
+        return carry
+
+    lax.fori_loop(1, devices, coef_sent, 0)
+    row3 = lax.broadcasted_iota(jnp.int32, (2 * group, 2 * group), 0)
+    col3 = lax.broadcasted_iota(jnp.int32, (2 * group, 2 * group), 1)
+    slot3 = row3 % group
+    want = (slot3 // share) * (2 * share) + (row3 // group) * share + slot3 % share
+    sort = jnp.where(col3 == want, 1.0, 0.0).astype(bf16)
+    for copy in copies:
+        copy.wait()
+    low = solved_all[...].reshape(2 * group, vecs).astype(bf16)
+    low = jnp.dot(sort, low, preferred_element_type=f32).astype(bf16)
+    for copy in packs + defls:
+        copy.wait()
+    for i in range(sites_here):
+        z = jnp.dot(low, gathered[i], preferred_element_type=f32)
+        start = (z[:group] + lanes_turned(z[group:], False)).astype(bf16)
+        ext0[reach + i] = start
+        sol_ref[i] = start.astype(f32)
+
+    def halo(step):
+        buf = exts[step]
+        up = pltpu.make_async_remote_copy(
+            src_ref=buf.at[pl.ds(sites_here, reach)], dst_ref=buf.at[pl.ds(0, reach)],
+            send_sem=halo_send.at[2 * step], recv_sem=halo_recv.at[2 * step],
+            device_id=(along(1), my_rhs), device_id_type=MESH)
+        down = pltpu.make_async_remote_copy(
+            src_ref=buf.at[pl.ds(reach, reach)], dst_ref=buf.at[pl.ds(reach + sites_here, reach)],
+            send_sem=halo_send.at[2 * step + 1], recv_sem=halo_recv.at[2 * step + 1],
+            device_id=(along(n_site - 1), my_rhs), device_id_type=MESH)
+        up.start()
+        down.start()
+        return up, down
+
+    anchor = my_site * sites_here - reach
+
+    def operate(step, i):
+        pieces = [exts[step][reach + i]]
+        for m in range(nb_ref.shape[1]):
+            at = (nb_ref[i, m] - anchor) & (2 * sites_here - 1)
+            pieces.append(exts[step][at])
+        stacked = jnp.concatenate(pieces, axis=1)
+        return jnp.dot(stacked, coup[i], preferred_element_type=f32)
+
+    copies = halo(0)
+    load_coup.wait()
+    for copy in copies:
+        copy.wait()
+    for i in range(sites_here):
+        r = given[i].astype(f32) - operate(0, i)
+        res_ref[i] = r
+        ext1[reach + i] = r.astype(bf16)
+
+    lane = lax.broadcasted_iota(jnp.int32, (8, width), 1)
+    bands = group // 8
+    for step in range(2):
+        for copy in halo(step + 1):
+            copy.wait()
+        tops = [jnp.zeros((group, width), f32) for _ in range(3)]
+        for i in range(sites_here):
+            y = operate(step + 1, i)
+            r = res_ref[i]
+            image[i] = y
+            tops[0] = tops[0] + y * r
+            tops[1] = tops[1] + y * lanes_turned(r, True)
+            tops[2] = tops[2] + y * y
+        tile = jnp.zeros((8, width), f32)
+        for v in range(3):
+            column = jnp.sum(tops[v], axis=1, keepdims=True)
+            for b in range(bands):
+                tile = jnp.where(lane == 3 * b + v, column[8 * b:8 * b + 8], tile)
+        sums[step] = tile
+        for copy in to_all_sites(sums.at[step], sums_all.at[step], sums_send.at[step], sums_recv.at[step]):
+            copy.wait()
+        tile = jnp.sum(sums_all[step], axis=0)
+        values = []
+        for v in range(3):
+            values.append(jnp.concatenate([tile[:, 3 * b + v:3 * b + v + 1] for b in range(bands)], axis=0))
+        alpha_re = values[0] / values[2]
+        alpha_im = values[1] / values[2]
+        for i in range(sites_here):
+            r, y = res_ref[i], image[i]
+            sol_ref[i] = sol_ref[i] + (alpha_re * r + alpha_im * lanes_turned(r, False))
+            r = r - (alpha_re * y + alpha_im * lanes_turned(y, False))
+            res_ref[i] = r
+            if step == 0:
+                ext2[reach + i] = r.astype(bf16)
+
+
+def fused(n_site, n_rhs, rhs_vecs, deflation, coarse_inverse, coupling, neighbours, grouping):
+    f32, bf16 = jnp.float32, jnp.bfloat16
+    slots, sites_local, width = rhs_vecs.shape
+    vecs = deflation.shape[0]
+    sites_here = coupling.shape[0]
+    group = slots // n_rhs
+    share = group // n_site
+    devices = n_site * n_rhs
+    blocks = coupling.reshape(sites_here, -1, width)
+    vmem = pl.BlockSpec(memory_space=pltpu.VMEM)
+    out = jax.ShapeDtypeStruct((sites_here, group, width), f32)
+    dma = pltpu.SemaphoreType.DMA
+    sol, res = pl.pallas_call(
+        functools.partial(fused_kernel, n_site, n_rhs),
+        out_shape=(out, out),
+        in_specs=[vmem, vmem, vmem, pl.BlockSpec(memory_space=pl.ANY),
+                  pl.BlockSpec(memory_space=pltpu.SMEM), vmem],
+        out_specs=(vmem, vmem),
+        scratch_shapes=[
+            pltpu.VMEM(blocks.shape, bf16),
+            pltpu.VMEM((sites_here, vecs, width), bf16),
+            pltpu.VMEM((sites_local, slots, width), bf16),
+            pltpu.VMEM((sites_here, group, width), bf16),
+            pltpu.VMEM((devices, 2 * share, vecs), f32),
+            pltpu.VMEM((devices, 2 * share, vecs), f32),
+            pltpu.VMEM((2 * share, vecs), f32),
+            pltpu.VMEM((n_site, 2 * share, vecs), f32),
+            pltpu.VMEM((2 * sites_here, group, width), bf16),
+            pltpu.VMEM((2 * sites_here, group, width), bf16),
+            pltpu.VMEM((2 * sites_here, group, width), bf16),
+            pltpu.VMEM((sites_here, group, width), f32),
+            pltpu.VMEM((2, 8, width), f32),
+            pltpu.VMEM((2, n_site, 8, width), f32),
+            dma, dma((devices,)), dma((devices,)), dma((n_rhs,)), dma((n_rhs,)),
+            dma((n_rhs,)), dma((n_rhs,)), dma((n_site,)), dma((n_site,)),
+            dma((6,)), dma((6,)), dma((2, n_site)), dma((2, n_site)),
+        ],
+        compiler_params=pltpu.CompilerParams(
+            collective_id=0, has_side_effects=True, vmem_limit_bytes=40 * 1024 * 1024),
+    )(
+        jnp.transpose(rhs_vecs, (1, 0, 2)),
+        jnp.transpose(deflation, (1, 0, 2)),
+        coarse_inverse,
+        blocks,
+        neighbours,
+        grouping.reshape(1, slots),
+    )
+    return jnp.transpose(sol, (1, 0, 2)), jnp.transpose(res, (1, 0, 2))
+
+
+def fits(n_site, n_rhs, rhs_vecs, coupling):
+    slots, sites_local, width = rhs_vecs.shape
+    sites_here = coupling.shape[0]
+    group = slots // n_rhs
+    share = group // n_site
+    return (
+        share * n_site * n_rhs == slots
+        and (2 * share) % 8 == 0
+        and group % 16 == 0
+        and 3 * (group // 8) <= width
+        and slots % 128 == 0
+        and width % 128 == 0
+        and sites_local * n_rhs == sites_here
+        and n_site >= 3
+        and n_site % 2 == 0
+        and sites_here & (sites_here - 1) == 0
+    )
+
+
+def per_device(n_site, n_rhs, *arrays):
+    if fits(n_site, n_rhs, arrays[0], arrays[3]):
+        return fused(n_site, n_rhs, *arrays)
+    return staged(*arrays)
+
+
 def solution(mesh):
     return jax.shard_map(
-        per_device,
+        functools.partial(per_device, mesh.shape["site"], mesh.shape["rhs"]),
         mesh=mesh,
         in_specs=(
             P(None, ("site", "rhs"), None),

time: 254 us -> 60.7 us (0.24)
  waiting for transfers between devices: 123 us -> 0 us
  blocking collectives: 54.1 us -> 0 us
  Pallas kernels: 0 us -> 51.4 us
  starting transfers between devices: 21.1 us -> 0 us
  matrix products: 19.7 us -> 0 us
  between operations: 14.2 us -> 0.66 us
  other arithmetic: 7.58 us -> 0 us
  local copies, waits for them, and re-layouts: 13.8 us -> 8.41 us
    psum x1 -> x0, waiting for transfers between devices: 73 us -> none  [per_device(): group_re, group_im = lax.psum((group_re, group_im), 'site')]
    pallas_call x0 -> x1, Pallas kernels: none -> 51.4 us  [fused(): pl.pallas_call(functools.partial(fused_kernel, n_site, n_rhs), out_shape=...]
    psum x2 -> x0, blocking collectives: 43.7 us -> none  [per_device(): upper_re, upper_im, lower = lax.psum((upper_re, upper_im, lower), 'site')]
    reduce_scatter x2 -> x0, waiting for transfers between devices: 42.7 us -> none  [the longest x1 22.6 us: per_device(): lax.psum_scatter(coef_im, 'rhs', scatter_dimension=1, tiled=True)]
    dot_general x11 -> x0, matrix products: 19.7 us -> none  [the longest x3 11.1 us: operate(): lax.dot_general(stacked, blocks, (((2,), (1,)), ((1,), (0,))), preferred_...]
    ppermute x6 -> x0, starting transfers between devices: 14.3 us -> none  [the longest x3 11.5 us: extended_2(): after = lax.ppermute(first, axis, down)]
    all_gather x2 -> x0, blocking collectives: 10.5 us -> none  [the longest x1 5.24 us: per_device(): lax.all_gather(share_im.astype(jnp.bfloat16), 'rhs', axis=1, tiled=True)]
    all_to_all x2 -> x0, starting transfers between devices: 6.65 us -> none  [the longest x1 3.33 us: per_device(): lax.all_to_all(ordered, 'rhs', split_axis=0, concat_axis=1, tiled=True)]
  transfers between devices with their start and end apart: 11 -> 0, of which waited for: 7 -> 0; matrix products, arithmetic and copies ran while one was open for 3% -> 0% of each run, Pallas kernels for 0% -> 0%
where the time goes in v1:
time: 60.7 us; the launch traced here: 60.5 us
  Pallas kernels  51.4 us (85%)
  local copies, waits for them, and re-layouts  8.41 us (14%)
  between operations  0.66 us (1%)
    pallas_call x1, Pallas kernels, fused(): pl.pallas_call(functools.partial(fused_kernel, n_site, n_rhs), out_shape=...  51.4 us
    unnamed x11, local copies, waits for them, and re-layouts  8.41 us

profile of v1, /device:TPU:0, one launch (start us, length us, event | category | flops | bytes accessed | tf_op | source)
XLA Modules:
  0.0 60.5 jit_solution(13976891118037185781)
XLA Ops:
  0.6 0.8 %copy.10.nb_ref = s32[16,8]{1,0:T(8,128)S(1)} copy(s32[16,8]{0,1:T(8,128)} %param.10) | data formatting | bytes 1024 | tf_op args[4]
  1.4 0.9 %copy.16 = bf16[128,4,128]{2,0,1:T(8,128)(2,1)S(1)} copy(bf16[128,4,128]{2,1,0:T(4,128)(2,1)} %param.6) | data formatting | bytes 262144 | tf_op args[0]
  2.3 1.0 %copy.15 = bf16[256,4,128]{2,0,1:T(8,128)(2,1)S(1)} copy(bf16[256,4,128]{2,1,0:T(4,128)(2,1)} %param.7) | data formatting | bytes 524288 | tf_op args[1]
  3.3 0.0 copy-start
  3.3 2.3 %copy-done = bf16[16,9,128,128]{3,2,1,0:T(8,128)(2,1)S(1)} copy-done((bf16[16,9,128,128]{3,2,1,0:T(8,128)(2,1)S(1)}, bf16[16,9,128,128]{3,2,1,0:T(8,128)(2,1)}, u32[]{:S(2)}) %copy-start) | copy-done | bytes 4718616
  5.6 0.0 copy-start.1
  5.6 1.0 %copy-done.1 = f32[2,256,256]{2,1,0:T(8,128)S(1)} copy-done((f32[2,256,256]{2,1,0:T(8,128)S(1)}, f32[2,256,256]{2,1,0:T(8,128)}, u32[]{:S(2)}) %copy-start.1) | copy-done | bytes 524312
  6.7 0.0 copy-start.2
  6.7 0.7 %copy-done.2 = s32[128]{0:T(128)S(1)} copy-done((s32[128]{0:T(128)S(1)}, s32[128]{0:T(128)}, u32[]{:S(2)}) %copy-start.2) | copy-done | bytes 536
  7.3 51.4 %shard_map.77 = (f32[16,32,128]{2,1,0:T(8,128)S(1)}, f32[16,32,128]{2,1,0:T(8,128)S(1)}) custom-call(bf16[4,128,128]{2,1,0:T(8,128)(2,1)S(1)} %bitcast.12, bf16[4,256,128]{2,1,0:T(8,128)(2,1)S(1)} %bitcast.11, f32[2,256,256]{2,1,0:T(8,128)S(1)} %copy-done.1, bf16[16,1152,128]{2,1,0:T(8,128)(2,1)S(1)} %bitcast.10, s32[16,8]{1,0:T(8,128)S(1)} %copy.10.nb_ref, ...), custom_call_target="tpu_custom_call" | custom-call | tf_op jit(solution)/shard_map/pallas_call | solution.py:355
  58.7 0.9 %copy.11 = f32[32,16,128]{2,1,0:T(8,128)} copy(f32[32,16,128]{2,0,1:T(8,128)S(1)} %bitcast.14) | data formatting | bytes 524288
  59.6 0.9 %copy.12 = f32[32,16,128]{2,1,0:T(8,128)} copy(f32[32,16,128]{2,0,1:T(8,128)S(1)} %bitcast.13) | data formatting | bytes 524288
Async XLA Ops:
  3.3 2.3 %copy-start = (bf16[16,9,128,128]{3,2,1,0:T(8,128)(2,1)S(1)}, bf16[16,9,128,128]{3,2,1,0:T(8,128)(2,1)}, u32[]{:S(2)}) copy-start(bf16[16,9,128,128]{3,2,1,0:T(8,128)(2,1)} %param.9) | copy-start | bytes 14155780
  5.6 1.0 %copy-start.1 = (f32[2,256,256]{2,1,0:T(8,128)S(1)}, f32[2,256,256]{2,1,0:T(8,128)}, u32[]{:S(2)}) copy-start(f32[2,256,256]{2,1,0:T(8,128)} %inv_ref.1) | copy-start | bytes 1572868
  6.7 0.7 %copy-start.2 = (s32[128]{0:T(128)S(1)}, s32[128]{0:T(128)}, u32[]{:S(2)}) copy-start(s32[128]{0:T(128)} %param.11) | copy-start | bytes 1540

commit v2 on v1

--- a/solution.py
+++ b/solution.py
@@ -130,19 +130,21 @@
 
 def fused_kernel(
     n_site, n_rhs,
-    rhs_ref, defl_ref, inv_ref, coup_hbm, nb_ref, group_ref,
+    rhs_hbm, defl_hbm, inv_hbm, coup_hbm, nb_hbm, group_ref,
     sol_ref, res_ref,
-    coup, gathered, ordered, given, coef, parts, solved, solved_all, ext0, ext1, ext2, image, sums, sums_all,
-    coup_sem, coef_send, coef_recv, pack_send, pack_recv, defl_send, defl_recv,
+    rhs_ref, defl_ref, wide, inv, nb, coup, gathered, ordered, given, coef, parts, solved, solved_all, ext0, ext1, ext2, image, sums, sums_all,
+    rhs_sem, defl_sem, inv_sem, nb_sem, coup_sem, coef_send, coef_recv, pack_send, pack_recv, defl_send, defl_recv,
     solved_send, solved_recv, halo_send, halo_recv, sums_send, sums_recv,
 ):
     devices = n_site * n_rhs
-    sites_local, slots, width = rhs_ref.shape
+    width = rhs_ref.shape[1]
+    slots = group_ref.shape[1]
+    sites_local = rhs_ref.shape[0] // slots
     sites_here = coup_hbm.shape[0]
     reach = sites_here // 2
     group = slots // n_rhs
     share = group // n_site
-    vecs = defl_ref.shape[1]
+    vecs = inv_hbm.shape[1]
     f32, bf16 = jnp.float32, jnp.bfloat16
     exts = (ext0, ext1, ext2)
 
@@ -154,6 +156,16 @@
         at = lax.rem(me + d, devices)
         return at, (lax.rem(at, n_site), at // n_site)
 
+    load_coup = pltpu.make_async_copy(coup_hbm, coup, coup_sem)
+    load_nb = pltpu.make_async_copy(nb_hbm, nb, nb_sem)
+    load_inv = pltpu.make_async_copy(inv_hbm, inv, inv_sem)
+    load_rhs = pltpu.make_async_copy(rhs_hbm, rhs_ref, rhs_sem)
+    load_defl = pltpu.make_async_copy(defl_hbm, defl_ref, defl_sem)
+    load_defl.start()
+    load_rhs.start()
+    load_nb.start()
+    load_inv.start()
+    load_coup.start()
     barrier = pltpu.get_barrier_semaphore()
 
     def greet(d, carry):
@@ -162,26 +174,34 @@
         return carry
 
     lax.fori_loop(1, devices, greet, 0)
-    load_coup = pltpu.make_async_copy(coup_hbm, coup, coup_sem)
-    load_coup.start()
-
-    row = lax.broadcasted_iota(jnp.int32, (slots, slots), 0)
-    placed = jnp.where(row == group_ref[...], 1.0, 0.0).astype(f32)
-    placed = jnp.transpose(placed).astype(bf16)
+    own = my_rhs * sites_local
+    load_defl.wait()
+    wide[...] = defl_ref[...].astype(f32)
+    basis = []
+    for i in range(sites_local):
+        block = wide[pl.ds(i, vecs, stride=sites_local), :].astype(bf16)
+        gathered[own + i] = block
+        basis.append(block)
+    basis = jnp.concatenate(basis, axis=1)
+
+    row = lax.broadcasted_iota(jnp.int32, (slots * sites_local, slots), 0)
+    wanted = group_ref[...] * sites_local
+    tn = (((0,), (0,)), ((), ()))
     row2 = lax.broadcasted_iota(jnp.int32, (2 * slots, slots), 0)
     col2 = lax.broadcasted_iota(jnp.int32, (2 * slots, slots), 1)
     spread = jnp.where(col2 == (row2 // (2 * share)) * share + row2 % share, 1.0, 0.0).astype(bf16)
     part = (lax.broadcasted_iota(jnp.int32, (2 * slots, width), 0) // share) % 2
     both = []
+    load_rhs.wait()
     for i in range(sites_local):
-        g = jnp.dot(placed, rhs_ref[i], preferred_element_type=f32).astype(bf16)
+        placed = jnp.where(row == wanted + i, 1.0, 0.0).astype(bf16)
+        g = lax.dot_general(placed, rhs_ref[...], tn, preferred_element_type=f32).astype(bf16)
         ordered[i] = g
         two = jnp.dot(spread, g, preferred_element_type=f32)
         both.append(jnp.where(part == 1, lanes_turned(two, True), two).astype(bf16))
     both = jnp.concatenate(both, axis=1)
-    basis = jnp.concatenate([defl_ref[i] for i in range(sites_local)], axis=1)
     total = lax.dot_general(both, basis, (((1,), (1,)), ((), ())), preferred_element_type=f32)
-    coef[...] = total.reshape(devices, 2 * share, vecs)
+    coef[...] = total.reshape(devices, 2 * share, vecs).astype(bf16)
 
     pl.semaphore_wait(barrier, devices - 1)
 
@@ -202,18 +222,17 @@
         other = lax.rem(my_rhs + d, n_rhs)
         packs.append(pltpu.make_async_remote_copy(
             src_ref=ordered.at[:, pl.ds(pl.multiple_of(other * group, group), group), :],
-            dst_ref=given.at[pl.ds(my_rhs * sites_local, sites_local)],
+            dst_ref=given.at[pl.ds(own, sites_local)],
             send_sem=pack_send.at[d], recv_sem=pack_recv.at[d],
             device_id=(my_site, other), device_id_type=MESH))
         defls.append(pltpu.make_async_remote_copy(
-            src_ref=defl_ref,
-            dst_ref=gathered.at[pl.ds(my_rhs * sites_local, sites_local)],
+            src_ref=gathered.at[pl.ds(own, sites_local)],
+            dst_ref=gathered.at[pl.ds(own, sites_local)],
             send_sem=defl_send.at[d], recv_sem=defl_recv.at[d],
             device_id=(my_site, other), device_id_type=MESH))
     for copy in packs + defls:
         copy.start()
-    given[pl.ds(my_rhs * sites_local, sites_local)] = ordered[:, pl.ds(pl.multiple_of(my_rhs * group, group), group), :]
-    gathered[pl.ds(my_rhs * sites_local, sites_local)] = defl_ref[...]
+    given[pl.ds(own, sites_local)] = ordered[:, pl.ds(pl.multiple_of(my_rhs * group, group), group), :]
     parts[me] = coef[me]
 
     def coef_wait(d, carry):
@@ -224,14 +243,15 @@
         return carry
 
     lax.fori_loop(1, devices, coef_wait, 0)
-    mine = jnp.sum(parts[...], axis=0)
+    mine = jnp.sum(parts[...].astype(f32), axis=0)
+    load_inv.wait()
     swapped = pltpu.roll(mine, share, 0)
     first = lax.broadcasted_iota(jnp.int32, mine.shape, 0) < share
     swapped = jnp.where(first, -swapped, swapped)
     nt = (((1,), (1,)), ((), ()))
-    out = lax.dot_general(mine, inv_ref[0], nt, precision=lax.Precision.HIGHEST, preferred_element_type=f32)
-    out = out + lax.dot_general(swapped, inv_ref[1], nt, precision=lax.Precision.HIGHEST, preferred_element_type=f32)
-    solved[...] = out
+    out = lax.dot_general(mine, inv[0], nt, precision=lax.Precision.HIGHEST, preferred_element_type=f32)
+    out = out + lax.dot_general(swapped, inv[1], nt, precision=lax.Precision.HIGHEST, preferred_element_type=f32)
+    solved[...] = out.astype(bf16)
 
     def along(d):
         return lax.rem(my_site + d, n_site)
@@ -261,7 +281,7 @@
     sort = jnp.where(col3 == want, 1.0, 0.0).astype(bf16)
     for copy in copies:
         copy.wait()
-    low = solved_all[...].reshape(2 * group, vecs).astype(bf16)
+    low = solved_all[...].astype(f32).reshape(2 * group, vecs).astype(bf16)
     low = jnp.dot(sort, low, preferred_element_type=f32).astype(bf16)
     for copy in packs + defls:
         copy.wait()
@@ -289,13 +309,14 @@
 
     def operate(step, i):
         pieces = [exts[step][reach + i]]
-        for m in range(nb_ref.shape[1]):
-            at = (nb_ref[i, m] - anchor) & (2 * sites_here - 1)
+        for m in range(nb.shape[0]):
+            at = (nb[m, i] - anchor) & (2 * sites_here - 1)
             pieces.append(exts[step][at])
         stacked = jnp.concatenate(pieces, axis=1)
         return jnp.dot(stacked, coup[i], preferred_element_type=f32)
 
     copies = halo(0)
+    load_nb.wait()
     load_coup.wait()
     for copy in copies:
         copy.wait()
@@ -350,41 +371,46 @@
     devices = n_site * n_rhs
     blocks = coupling.reshape(sites_here, -1, width)
     vmem = pl.BlockSpec(memory_space=pltpu.VMEM)
+    hbm = pl.BlockSpec(memory_space=pltpu.HBM)
     out = jax.ShapeDtypeStruct((sites_here, group, width), f32)
     dma = pltpu.SemaphoreType.DMA
     sol, res = pl.pallas_call(
         functools.partial(fused_kernel, n_site, n_rhs),
         out_shape=(out, out),
-        in_specs=[vmem, vmem, vmem, pl.BlockSpec(memory_space=pl.ANY),
-                  pl.BlockSpec(memory_space=pltpu.SMEM), vmem],
+        in_specs=[hbm, hbm, hbm, hbm, hbm, vmem],
         out_specs=(vmem, vmem),
         scratch_shapes=[
+            pltpu.VMEM((slots * sites_local, width), bf16),
+            pltpu.VMEM((vecs * sites_local, width), bf16),
+            pltpu.VMEM((vecs * sites_local, width), f32),
+            pltpu.VMEM(coarse_inverse.shape, f32),
+            pltpu.SMEM(neighbours.shape[::-1], jnp.int32),
             pltpu.VMEM(blocks.shape, bf16),
             pltpu.VMEM((sites_here, vecs, width), bf16),
             pltpu.VMEM((sites_local, slots, width), bf16),
             pltpu.VMEM((sites_here, group, width), bf16),
-            pltpu.VMEM((devices, 2 * share, vecs), f32),
-            pltpu.VMEM((devices, 2 * share, vecs), f32),
-            pltpu.VMEM((2 * share, vecs), f32),
-            pltpu.VMEM((n_site, 2 * share, vecs), f32),
+            pltpu.VMEM((devices, 2 * share, vecs), bf16),
+            pltpu.VMEM((devices, 2 * share, vecs), bf16),
+            pltpu.VMEM((2 * share, vecs), bf16),
+            pltpu.VMEM((n_site, 2 * share, vecs), bf16),
             pltpu.VMEM((2 * sites_here, group, width), bf16),
             pltpu.VMEM((2 * sites_here, group, width), bf16),
             pltpu.VMEM((2 * sites_here, group, width), bf16),
             pltpu.VMEM((sites_here, group, width), f32),
             pltpu.VMEM((2, 8, width), f32),
             pltpu.VMEM((2, n_site, 8, width), f32),
-            dma, dma((devices,)), dma((devices,)), dma((n_rhs,)), dma((n_rhs,)),
+            dma, dma, dma, dma, dma, dma((devices,)), dma((devices,)), dma((n_rhs,)), dma((n_rhs,)),
             dma((n_rhs,)), dma((n_rhs,)), dma((n_site,)), dma((n_site,)),
             dma((6,)), dma((6,)), dma((2, n_site)), dma((2, n_site)),
         ],
         compiler_params=pltpu.CompilerParams(
-            collective_id=0, has_side_effects=True, vmem_limit_bytes=40 * 1024 * 1024),
+            collective_id=0, has_side_effects=True, vmem_limit_bytes=63 * 1024 * 1024),
     )(
-        jnp.transpose(rhs_vecs, (1, 0, 2)),
-        jnp.transpose(deflation, (1, 0, 2)),
+        rhs_vecs.reshape(slots * sites_local, width),
+        deflation.reshape(vecs * sites_local, width),
         coarse_inverse,
         blocks,
-        neighbours,
+        neighbours.T,
         grouping.reshape(1, slots),
     )
     return jnp.transpose(sol, (1, 0, 2)), jnp.transpose(res, (1, 0, 2))

time: 60.7 us -> 55 us (0.906)
  local copies, waits for them, and re-layouts: 8.41 us -> 3.62 us
  Pallas kernels: 51.4 us -> 50.5 us
    unnamed x11 -> x2, local copies, waits for them, and re-layouts: 8.41 us -> 3.62 us
    pallas_call x1, Pallas kernels: 51.4 us -> 50.5 us  [fused(): pl.pallas_call(functools.partial(fused_kernel, n_site, n_rhs), out_shape=...]
where the time goes in v2:
time: 55 us; the launch traced here: 54.8 us
  Pallas kernels  50.5 us (92%)
  local copies, waits for them, and re-layouts  3.62 us (7%)
  between operations  0.64 us (1%)
    pallas_call x1, Pallas kernels, fused(): pl.pallas_call(functools.partial(fused_kernel, n_site, n_rhs), out_shape=...  50.5 us
    unnamed x2, local copies, waits for them, and re-layouts  3.62 us

profile of v2, /device:TPU:0, one launch (start us, length us, event | category | flops | bytes accessed | tf_op | source)
XLA Modules:
  0.0 54.8 jit_solution(2204296661663658774)
XLA Ops:
  0.6 50.5 %shard_map.77 = (f32[16,32,128]{2,1,0:T(8,128)}, f32[16,32,128]{2,1,0:T(8,128)}) custom-call(bf16[512,128]{1,0:T(8,128)(2,1)} %bitcast.11, bf16[1024,128]{1,0:T(8,128)(2,1)} %bitcast.8, f32[2,256,256]{2,1,0:T(8,128)} %inv_hbm.1, bf16[16,1152,128]{2,1,0:T(8,128)(2,1)} %bitcast.7, s32[8,16]{1,0:T(8,128)} %bitcast.12, s32[1,128]{1,0:T(1,128)} %bitcast.13), custom_call_target="tpu_custom_call" | custom-call | tf_op jit(solution)/shard_map/pallas_call | solution.py:377
  51.2 1.8 %copy.8 = f32[32,16,128]{2,1,0:T(8,128)} copy(f32[32,16,128]{2,0,1:T(8,128)} %bitcast.10) | data formatting | bytes 524288
  53.0 1.8 %copy.9 = f32[32,16,128]{2,1,0:T(8,128)} copy(f32[32,16,128]{2,0,1:T(8,128)} %bitcast.9) | data formatting | bytes 524288

commit v3 on v2

--- a/solution.py
+++ b/solution.py
@@ -132,7 +132,7 @@
     n_site, n_rhs,
     rhs_hbm, defl_hbm, inv_hbm, coup_hbm, nb_hbm, group_ref,
     sol_ref, res_ref,
-    rhs_ref, defl_ref, wide, inv, nb, coup, gathered, ordered, given, coef, parts, solved, solved_all, ext0, ext1, ext2, image, sums, sums_all,
+    rhs_ref, defl_ref, wide, inv, nb, coup, gathered, ordered, given, coef, parts, solved, solved_all, low0, high0, low1, high1, low2, high2, low3, high3, first_res, image, sums, sums_all,
     rhs_sem, defl_sem, inv_sem, nb_sem, coup_sem, coef_send, coef_recv, pack_send, pack_recv, defl_send, defl_recv,
     solved_send, solved_recv, halo_send, halo_recv, sums_send, sums_recv,
 ):
@@ -146,7 +146,7 @@
     share = group // n_site
     vecs = inv_hbm.shape[1]
     f32, bf16 = jnp.float32, jnp.bfloat16
-    exts = (ext0, ext1, ext2)
+    bufs = ((low0, high0), (low1, high1), (low2, high2), (low3, high3))
 
     my_site = lax.axis_index("site")
     my_rhs = lax.axis_index("rhs")
@@ -285,80 +285,121 @@
     low = jnp.dot(sort, low, preferred_element_type=f32).astype(bf16)
     for copy in packs + defls:
         copy.wait()
-    for i in range(sites_here):
-        z = jnp.dot(low, gathered[i], preferred_element_type=f32)
-        start = (z[:group] + lanes_turned(z[group:], False)).astype(bf16)
-        ext0[reach + i] = start
-        sol_ref[i] = start.astype(f32)
-
-    def halo(step):
-        buf = exts[step]
-        up = pltpu.make_async_remote_copy(
-            src_ref=buf.at[pl.ds(sites_here, reach)], dst_ref=buf.at[pl.ds(0, reach)],
-            send_sem=halo_send.at[2 * step], recv_sem=halo_recv.at[2 * step],
-            device_id=(along(1), my_rhs), device_id_type=MESH)
-        down = pltpu.make_async_remote_copy(
-            src_ref=buf.at[pl.ds(reach, reach)], dst_ref=buf.at[pl.ds(reach + sites_here, reach)],
-            send_sem=halo_send.at[2 * step + 1], recv_sem=halo_recv.at[2 * step + 1],
-            device_id=(along(n_site - 1), my_rhs), device_id_type=MESH)
-        up.start()
-        down.start()
-        return up, down
-
     anchor = my_site * sites_here - reach
+    halves = (range(reach), range(reach, sites_here))
+
+    def keep(step, i, values):
+        for buf in bufs[step]:
+            buf[reach + i] = values
+
+    def halo(step, half):
+        own_buf, out_buf = bufs[step]
+        if half == 0:
+            source, target, to = out_buf.at[pl.ds(reach, reach)], out_buf.at[pl.ds(reach + sites_here, reach)], n_site - 1
+        else:
+            source, target, to = own_buf.at[pl.ds(sites_here, reach)], own_buf.at[pl.ds(0, reach)], 1
+        copy = pltpu.make_async_remote_copy(
+            src_ref=source, dst_ref=target,
+            send_sem=halo_send.at[2 * step + half], recv_sem=halo_recv.at[2 * step + half],
+            device_id=(along(to), my_rhs), device_id_type=MESH)
+        copy.start()
+        return copy
 
     def operate(step, i):
-        pieces = [exts[step][reach + i]]
+        buf = bufs[step][i // reach]
+        pieces = [buf[reach + i]]
         for m in range(nb.shape[0]):
-            at = (nb[m, i] - anchor) & (2 * sites_here - 1)
-            pieces.append(exts[step][at])
+            pieces.append(buf[(nb[m, i] - anchor) & (2 * sites_here - 1)])
         stacked = jnp.concatenate(pieces, axis=1)
         return jnp.dot(stacked, coup[i], preferred_element_type=f32)
 
-    copies = halo(0)
+    copies = []
+    for half in (0, 1):
+        for i in halves[half]:
+            z = jnp.dot(low, gathered[i], preferred_element_type=f32)
+            start = (z[:group] + lanes_turned(z[group:], False)).astype(bf16)
+            keep(0, i, start)
+            sol_ref[i] = start.astype(f32)
+        copies.append(halo(0, half))
     load_nb.wait()
     load_coup.wait()
-    for copy in copies:
-        copy.wait()
-    for i in range(sites_here):
-        r = given[i].astype(f32) - operate(0, i)
-        res_ref[i] = r
-        ext1[reach + i] = r.astype(bf16)
+    later = [None, None]
+    for half in (1, 0):
+        copies[1 - half].wait_recv()
+        for i in halves[half]:
+            r = given[i].astype(f32) - operate(0, i)
+            first_res[i] = r
+            keep(1, i, r.astype(bf16))
+        later[half] = halo(1, half)
+    sent = copies + later
 
     lane = lax.broadcasted_iota(jnp.int32, (8, width), 1)
     bands = group // 8
-    for step in range(2):
-        for copy in halo(step + 1):
-            copy.wait()
-        tops = [jnp.zeros((group, width), f32) for _ in range(3)]
-        for i in range(sites_here):
-            y = operate(step + 1, i)
-            r = res_ref[i]
-            image[i] = y
+
+    def apply(step, half, held, into, tops, low_too):
+        for i in halves[half]:
+            y = operate(step, i)
+            r = held[i]
+            into[i] = y
+            if low_too:
+                keep(2, i, y.astype(bf16))
             tops[0] = tops[0] + y * r
             tops[1] = tops[1] + y * lanes_turned(r, True)
             tops[2] = tops[2] + y * y
+
+    def send_sums(step, tops):
         tile = jnp.zeros((8, width), f32)
         for v in range(3):
             column = jnp.sum(tops[v], axis=1, keepdims=True)
             for b in range(bands):
                 tile = jnp.where(lane == 3 * b + v, column[8 * b:8 * b + 8], tile)
         sums[step] = tile
-        for copy in to_all_sites(sums.at[step], sums_all.at[step], sums_send.at[step], sums_recv.at[step]):
+        return to_all_sites(sums.at[step], sums_all.at[step], sums_send.at[step], sums_recv.at[step])
+
+    def alphas(step, waits):
+        for copy in waits:
             copy.wait()
         tile = jnp.sum(sums_all[step], axis=0)
         values = []
         for v in range(3):
             values.append(jnp.concatenate([tile[:, 3 * b + v:3 * b + v + 1] for b in range(bands)], axis=0))
-        alpha_re = values[0] / values[2]
-        alpha_im = values[1] / values[2]
-        for i in range(sites_here):
-            r, y = res_ref[i], image[i]
-            sol_ref[i] = sol_ref[i] + (alpha_re * r + alpha_im * lanes_turned(r, False))
-            r = r - (alpha_re * y + alpha_im * lanes_turned(y, False))
-            res_ref[i] = r
-            if step == 0:
-                ext2[reach + i] = r.astype(bf16)
+        alpha_re = jnp.broadcast_to(values[0] / values[2], (group, width))
+        alpha_im = jnp.broadcast_to(values[1] / values[2], (group, width))
+        return lambda vectors: alpha_re * vectors + alpha_im * lanes_turned(vectors, False)
+
+    tops = [jnp.zeros((group, width), f32) for _ in range(3)]
+    beside = []
+    for half in (0, 1):
+        later[1 - half].wait_recv()
+        apply(1, half, first_res, image, tops, True)
+        if half == 0:
+            beside.append(halo(2, 0))
+    waits = send_sums(0, tops)
+    beside.append(halo(2, 1))
+    first_scaled = alphas(0, waits)
+    for i in range(sites_here):
+        r = first_res[i] - first_scaled(image[i])
+        res_ref[i] = r
+        keep(3, i, r.astype(bf16))
+    for half in (1, 0):
+        beside[1 - half].wait_recv()
+        at = (0, reach + sites_here)[half]
+        for i in range(reach):
+            r = bufs[1][half][at + i].astype(f32) - first_scaled(bufs[2][half][at + i].astype(f32))
+            bufs[3][half][at + i] = r.astype(bf16)
+    tops = [jnp.zeros((group, width), f32) for _ in range(3)]
+    for half in (1, 0):
+        apply(3, half, res_ref, image, tops, False)
+    waits = send_sums(1, tops)
+    for i in range(sites_here):
+        sol_ref[i] = sol_ref[i] + first_scaled(first_res[i])
+    for copy in sent + beside:
+        copy.wait_send()
+    second_scaled = alphas(1, waits)
+    for i in range(sites_here):
+        r = res_ref[i]
+        sol_ref[i] = sol_ref[i] + second_scaled(r)
+        res_ref[i] = r - second_scaled(image[i])
 
 
 def fused(n_site, n_rhs, rhs_vecs, deflation, coarse_inverse, coupling, neighbours, grouping):
@@ -396,6 +437,12 @@
             pltpu.VMEM((2 * sites_here, group, width), bf16),
             pltpu.VMEM((2 * sites_here, group, width), bf16),
             pltpu.VMEM((2 * sites_here, group, width), bf16),
+            pltpu.VMEM((2 * sites_here, group, width), bf16),
+            pltpu.VMEM((2 * sites_here, group, width), bf16),
+            pltpu.VMEM((2 * sites_here, group, width), bf16),
+            pltpu.VMEM((2 * sites_here, group, width), bf16),
+            pltpu.VMEM((2 * sites_here, group, width), bf16),
+            pltpu.VMEM((sites_here, group, width), f32),
             pltpu.VMEM((sites_here, group, width), f32),
             pltpu.VMEM((2, 8, width), f32),
             pltpu.VMEM((2, n_site, 8, width), f32),

time: 55 us -> 50.8 us (0.924)
  Pallas kernels: 50.5 us -> 46.4 us
    pallas_call x1, Pallas kernels: 50.5 us -> 46.4 us  [fused(): pl.pallas_call(functools.partial(fused_kernel, n_site, n_rhs), out_shape=...]
where the time goes in v3:
time: 50.8 us; the launch traced here: 50.7 us
  Pallas kernels  46.4 us (91%)
  local copies, waits for them, and re-layouts  3.62 us (7%)
  between operations  0.64 us (1%)
    pallas_call x1, Pallas kernels, fused(): pl.pallas_call(functools.partial(fused_kernel, n_site, n_rhs), out_shape=...  46.4 us
    unnamed x2, local copies, waits for them, and re-layouts  3.62 us

profile of v3, /device:TPU:0, one launch (start us, length us, event | category | flops | bytes accessed | tf_op | source)
XLA Modules:
  0.0 50.7 jit_solution(16006244683760604249)
XLA Ops:
  0.6 46.4 %shard_map.77 = (f32[16,32,128]{2,1,0:T(8,128)}, f32[16,32,128]{2,1,0:T(8,128)}) custom-call(bf16[512,128]{1,0:T(8,128)(2,1)} %bitcast.11, bf16[1024,128]{1,0:T(8,128)(2,1)} %bitcast.8, f32[2,256,256]{2,1,0:T(8,128)} %inv_hbm.1, bf16[16,1152,128]{2,1,0:T(8,128)(2,1)} %bitcast.7, s32[8,16]{1,0:T(8,128)} %bitcast.12, s32[1,128]{1,0:T(1,128)} %bitcast.13), custom_call_target="tpu_custom_call" | custom-call | tf_op jit(solution)/shard_map/pallas_call | solution.py:418
  47.0 1.8 %copy.8 = f32[32,16,128]{2,1,0:T(8,128)} copy(f32[32,16,128]{2,0,1:T(8,128)} %bitcast.10) | data formatting | bytes 524288
  48.9 1.8 %copy.9 = f32[32,16,128]{2,1,0:T(8,128)} copy(f32[32,16,128]{2,0,1:T(8,128)} %bitcast.9) | data formatting | bytes 524288

commit v4 on v3

--- a/solution.py
+++ b/solution.py
@@ -217,19 +217,28 @@
 
     lax.fori_loop(1, devices, coef_start, 0)
 
+    def to_rhs(source, target, other, sends, recvs, d):
+        return pltpu.make_async_remote_copy(
+            src_ref=source, dst_ref=target, send_sem=sends.at[d], recv_sem=recvs.at[d],
+            device_id=(my_site, other), device_id_type=MESH)
+
+    half = n_rhs // 2
+    twin = my_rhs + 1 - 2 * lax.rem(my_rhs, 2)
+    mine_at = gathered.at[pl.ds(own, sites_local)]
     packs, defls = [], []
     for d in range(1, n_rhs):
         other = lax.rem(my_rhs + d, n_rhs)
-        packs.append(pltpu.make_async_remote_copy(
-            src_ref=ordered.at[:, pl.ds(pl.multiple_of(other * group, group), group), :],
-            dst_ref=given.at[pl.ds(own, sites_local)],
-            send_sem=pack_send.at[d], recv_sem=pack_recv.at[d],
-            device_id=(my_site, other), device_id_type=MESH))
-        defls.append(pltpu.make_async_remote_copy(
-            src_ref=gathered.at[pl.ds(own, sites_local)],
-            dst_ref=gathered.at[pl.ds(own, sites_local)],
-            send_sem=defl_send.at[d], recv_sem=defl_recv.at[d],
-            device_id=(my_site, other), device_id_type=MESH))
+        packs.append(to_rhs(
+            ordered.at[:, pl.ds(pl.multiple_of(other * group, group), group), :],
+            given.at[pl.ds(own, sites_local)], other, pack_send, pack_recv, d))
+    defls.append(to_rhs(mine_at, mine_at, twin, defl_send, defl_recv, 0))
+    relays = []
+    for d in range(1, half):
+        other = lax.rem(my_rhs + 2 * d, n_rhs)
+        defls.append(to_rhs(mine_at, mine_at, other, defl_send, defl_recv, d))
+        came = lax.rem(my_rhs + n_rhs - 2 * d, n_rhs) * sites_local
+        block = gathered.at[pl.ds(came, sites_local)]
+        relays.append(to_rhs(block, block, twin, defl_send, defl_recv, half + d))
     for copy in packs + defls:
         copy.start()
     given[pl.ds(own, sites_local)] = ordered[:, pl.ds(pl.multiple_of(my_rhs * group, group), group), :]
@@ -268,6 +277,9 @@
         return copies
 
     copies = to_all_sites(solved, solved_all, solved_send, solved_recv)
+    for copy, relay in zip(defls[1:], relays):
+        copy.wait_recv()
+        relay.start()
 
     def coef_sent(d, carry):
         coef_copy(d).wait_send()
@@ -283,8 +295,10 @@
         copy.wait()
     low = solved_all[...].astype(f32).reshape(2 * group, vecs).astype(bf16)
     low = jnp.dot(sort, low, preferred_element_type=f32).astype(bf16)
-    for copy in packs + defls:
+    for copy in packs + defls[:1] + relays:
         copy.wait()
+    for copy in defls[1:]:
+        copy.wait_send()
     anchor = my_site * sites_here - reach
     halves = (range(reach), range(reach, sites_here))
 
@@ -477,6 +491,7 @@
         and width % 128 == 0
         and sites_local * n_rhs == sites_here
         and n_site >= 3
+        and n_rhs % 2 == 0
         and n_site % 2 == 0
         and sites_here & (sites_here - 1) == 0
     )

time: 50.8 us -> 47 us (0.925)
  Pallas kernels: 46.4 us -> 42.5 us
    pallas_call x1, Pallas kernels: 46.4 us -> 42.5 us  [fused(): pl.pallas_call(functools.partial(fused_kernel, n_site, n_rhs), out_shape=...]
where the time goes in v4:
time: 47 us; the launch traced here: 46.8 us
  Pallas kernels  42.5 us (90%)
  local copies, waits for them, and re-layouts  3.62 us (8%)
  between operations  0.64 us (1%)
    pallas_call x1, Pallas kernels, fused(): pl.pallas_call(functools.partial(fused_kernel, n_site, n_rhs), out_shape=...  42.5 us
    unnamed x2, local copies, waits for them, and re-layouts  3.62 us

profile of v4, /device:TPU:0, one launch (start us, length us, event | category | flops | bytes accessed | tf_op | source)
XLA Modules:
  0.0 46.8 jit_solution(10546437598267235678)
XLA Ops:
  0.6 42.5 %shard_map.77 = (f32[16,32,128]{2,1,0:T(8,128)}, f32[16,32,128]{2,1,0:T(8,128)}) custom-call(bf16[512,128]{1,0:T(8,128)(2,1)} %bitcast.11, bf16[1024,128]{1,0:T(8,128)(2,1)} %bitcast.8, f32[2,256,256]{2,1,0:T(8,128)} %inv_hbm.1, bf16[16,1152,128]{2,1,0:T(8,128)(2,1)} %bitcast.7, s32[8,16]{1,0:T(8,128)} %bitcast.12, s32[1,128]{1,0:T(1,128)} %bitcast.13), custom_call_target="tpu_custom_call" | custom-call | tf_op jit(solution)/shard_map/pallas_call | solution.py:432
  43.2 1.8 %copy.8 = f32[32,16,128]{2,1,0:T(8,128)} copy(f32[32,16,128]{2,0,1:T(8,128)} %bitcast.10) | data formatting | bytes 524288
  45.0 1.8 %copy.9 = f32[32,16,128]{2,1,0:T(8,128)} copy(f32[32,16,128]{2,0,1:T(8,128)} %bitcast.9) | data formatting | bytes 524288

commit v5 on v4

--- a/solution.py
+++ b/solution.py
@@ -131,8 +131,8 @@
 def fused_kernel(
     n_site, n_rhs,
     rhs_hbm, defl_hbm, inv_hbm, coup_hbm, nb_hbm, group_ref,
-    sol_ref, res_ref,
-    rhs_ref, defl_ref, wide, inv, nb, coup, gathered, ordered, given, coef, parts, solved, solved_all, low0, high0, low1, high1, low2, high2, low3, high3, first_res, image, sums, sums_all,
+    sol_out, res_out,
+    sol_ref, res_ref, rhs_ref, defl_ref, wide, inv, nb, coup, gathered, ordered, given, coef, parts, solved, solved_all, low0, high0, low1, high1, low2, high2, low3, high3, first_res, image, sums, sums_all,
     rhs_sem, defl_sem, inv_sem, nb_sem, coup_sem, coef_send, coef_recv, pack_send, pack_recv, defl_send, defl_recv,
     solved_send, solved_recv, halo_send, halo_recv, sums_send, sums_recv,
 ):
@@ -412,8 +412,9 @@
     second_scaled = alphas(1, waits)
     for i in range(sites_here):
         r = res_ref[i]
-        sol_ref[i] = sol_ref[i] + second_scaled(r)
-        res_ref[i] = r - second_scaled(image[i])
+        rows = pl.ds(i, group, stride=sites_here)
+        sol_out[rows, :] = sol_ref[i] + second_scaled(r)
+        res_out[rows, :] = r - second_scaled(image[i])
 
 
 def fused(n_site, n_rhs, rhs_vecs, deflation, coarse_inverse, coupling, neighbours, grouping):
@@ -427,7 +428,7 @@
     blocks = coupling.reshape(sites_here, -1, width)
     vmem = pl.BlockSpec(memory_space=pltpu.VMEM)
     hbm = pl.BlockSpec(memory_space=pltpu.HBM)
-    out = jax.ShapeDtypeStruct((sites_here, group, width), f32)
+    out = pltpu.VMEM((group * sites_here, width), f32)
     dma = pltpu.SemaphoreType.DMA
     sol, res = pl.pallas_call(
         functools.partial(fused_kernel, n_site, n_rhs),
@@ -435,6 +436,8 @@
         in_specs=[hbm, hbm, hbm, hbm, hbm, vmem],
         out_specs=(vmem, vmem),
         scratch_shapes=[
+            pltpu.VMEM((sites_here, group, width), f32),
+            pltpu.VMEM((sites_here, group, width), f32),
             pltpu.VMEM((slots * sites_local, width), bf16),
             pltpu.VMEM((vecs * sites_local, width), bf16),
             pltpu.VMEM((vecs * sites_local, width), f32),
@@ -465,7 +468,7 @@
             dma((6,)), dma((6,)), dma((2, n_site)), dma((2, n_site)),
         ],
         compiler_params=pltpu.CompilerParams(
-            collective_id=0, has_side_effects=True, vmem_limit_bytes=63 * 1024 * 1024),
+            collective_id=0, has_side_effects=True, vmem_limit_bytes=62 * 1024 * 1024),
     )(
         rhs_vecs.reshape(slots * sites_local, width),
         deflation.reshape(vecs * sites_local, width),
@@ -474,7 +477,8 @@
         neighbours.T,
         grouping.reshape(1, slots),
     )
-    return jnp.transpose(sol, (1, 0, 2)), jnp.transpose(res, (1, 0, 2))
+    shape = (group, sites_here, width)
+    return sol.reshape(shape), res.reshape(shape)
 
 
 def fits(n_site, n_rhs, rhs_vecs, coupling):

time: 47 us -> 44 us (0.936)
  local copies, waits for them, and re-layouts: 3.62 us -> 1.41 us
  Pallas kernels: 42.5 us -> 41.8 us
    unnamed x2, local copies, waits for them, and re-layouts: 3.62 us -> 1.41 us
    pallas_call x1, Pallas kernels: 42.5 us -> 41.8 us  [fused(): pl.pallas_call(functools.partial(fused_kernel, n_site, n_rhs), out_shape=...]
where the time goes in v5:
time: 44 us; the launch traced here: 43.9 us
  Pallas kernels  41.8 us (95%)
  local copies, waits for them, and re-layouts  1.41 us (3%)
  between operations  0.64 us (1%)
    pallas_call x1, Pallas kernels, fused(): pl.pallas_call(functools.partial(fused_kernel, n_site, n_rhs), out_shape=...  41.8 us
    unnamed x2, local copies, waits for them, and re-layouts  1.41 us

profile of v5, /device:TPU:0, one launch (start us, length us, event | category | flops | bytes accessed | tf_op | source)
XLA Modules:
  0.0 43.9 jit_solution(3437837413850897126)
XLA Ops:
  0.6 41.8 %shard_map.77 = (f32[512,128]{1,0:T(8,128)S(1)}, f32[512,128]{1,0:T(8,128)S(1)}) custom-call(bf16[512,128]{1,0:T(8,128)(2,1)} %bitcast.11, bf16[1024,128]{1,0:T(8,128)(2,1)} %bitcast.10, f32[2,256,256]{2,1,0:T(8,128)} %inv_hbm.1, bf16[16,1152,128]{2,1,0:T(8,128)(2,1)} %bitcast.9, s32[8,16]{1,0:T(8,128)} %bitcast.12, s32[1,128]{1,0:T(1,128)} %bitcast.13), custom_call_target="tpu_custom_call" | custom-call | tf_op jit(solution)/shard_map/pallas_call | solution.py:433
  42.5 0.7 %copy.10 = f32[32,16,128]{2,1,0:T(8,128)} copy(f32[32,16,128]{2,1,0:T(8,128)S(1)} %bitcast.8) | data formatting | bytes 524288
  43.2 0.7 %copy.11 = f32[32,16,128]{2,1,0:T(8,128)} copy(f32[32,16,128]{2,1,0:T(8,128)S(1)} %bitcast.7) | data formatting | bytes 524288

commit v6 on v5

--- a/solution.py
+++ b/solution.py
@@ -173,7 +173,8 @@
         pl.semaphore_signal(barrier, inc=1, device_id=dev, device_id_type=MESH)
         return carry
 
-    lax.fori_loop(1, devices, greet, 0)
+    for d in range(1, devices):
+        greet(d, 0)
     own = my_rhs * sites_local
     load_defl.wait()
     wide[...] = defl_ref[...].astype(f32)
@@ -239,7 +240,7 @@
         came = lax.rem(my_rhs + n_rhs - 2 * d, n_rhs) * sites_local
         block = gathered.at[pl.ds(came, sites_local)]
         relays.append(to_rhs(block, block, twin, defl_send, defl_recv, half + d))
-    for copy in packs + defls:
+    for copy in defls[1:] + defls[:1] + packs:
         copy.start()
     given[pl.ds(own, sites_local)] = ordered[:, pl.ds(pl.multiple_of(my_rhs * group, group), group), :]
     parts[me] = coef[me]
@@ -295,7 +296,7 @@
         copy.wait()
     low = solved_all[...].astype(f32).reshape(2 * group, vecs).astype(bf16)
     low = jnp.dot(sort, low, preferred_element_type=f32).astype(bf16)
-    for copy in packs + defls[:1] + relays:
+    for copy in defls[:1] + relays:
         copy.wait()
     for copy in defls[1:]:
         copy.wait_send()
@@ -337,6 +338,8 @@
         copies.append(halo(0, half))
     load_nb.wait()
     load_coup.wait()
+    for copy in packs:
+        copy.wait()
     later = [None, None]
     for half in (1, 0):
         copies[1 - half].wait_recv()

time: 44 us -> 43.1 us (0.980)
  Pallas kernels: 41.8 us -> 40.8 us
    pallas_call x1, Pallas kernels: 41.8 us -> 40.8 us  [fused(): pl.pallas_call(functools.partial(fused_kernel, n_site, n_rhs), out_shape=...]
where the time goes in v6:
time: 43.1 us; the launch traced here: 42.9 us
  Pallas kernels  40.8 us (95%)
  local copies, waits for them, and re-layouts  1.41 us (3%)
  between operations  0.64 us (1%)
    pallas_call x1, Pallas kernels, fused(): pl.pallas_call(functools.partial(fused_kernel, n_site, n_rhs), out_shape=...  40.8 us
    unnamed x2, local copies, waits for them, and re-layouts  1.41 us

profile of v6, /device:TPU:0, one launch (start us, length us, event | category | flops | bytes accessed | tf_op | source)
XLA Modules:
  0.0 42.9 jit_solution(11431539492528894099)
XLA Ops:
  0.6 40.8 %shard_map.77 = (f32[512,128]{1,0:T(8,128)S(1)}, f32[512,128]{1,0:T(8,128)S(1)}) custom-call(bf16[512,128]{1,0:T(8,128)(2,1)} %bitcast.11, bf16[1024,128]{1,0:T(8,128)(2,1)} %bitcast.10, f32[2,256,256]{2,1,0:T(8,128)} %inv_hbm.1, bf16[16,1152,128]{2,1,0:T(8,128)(2,1)} %bitcast.9, s32[8,16]{1,0:T(8,128)} %bitcast.12, s32[1,128]{1,0:T(1,128)} %bitcast.13), custom_call_target="tpu_custom_call" | custom-call | tf_op jit(solution)/shard_map/pallas_call | solution.py:436
  41.5 0.7 %copy.10 = f32[32,16,128]{2,1,0:T(8,128)} copy(f32[32,16,128]{2,1,0:T(8,128)S(1)} %bitcast.8) | data formatting | bytes 524288
  42.2 0.7 %copy.11 = f32[32,16,128]{2,1,0:T(8,128)} copy(f32[32,16,128]{2,1,0:T(8,128)S(1)} %bitcast.7) | data formatting | bytes 524288
